TPU v7x, 32 devices: a whole 2x2x4 slice. The times are simulated.
32 devices in a mesh: groups: 2 (over x), example: 8 (over z, y), cls: 2 (over core).
Axes of the slice: x: 2, y: 2, z: 4, core: 2. Of those that a mesh axis runs over, the one named last changes fastest.
Arguments:
- features: bfloat16 [2048, 4096], P(('groups', 'example'), 'cls'), parts along dimension 0
- weights: float32 [8192, 8192], P(('groups', 'cls'), 'example'), parts along dimension 0
- labels: int32 [2048], P(('groups', 'example')), parts along dimension 0, may hold values from 0 to 8191
- counts: int32 [16], P(('groups', 'example')), parts along dimension 0, may hold values from 16 to 128, as said below
- active: int32 [2], P('groups'), parts along dimension 0, may hold values from 4096 to 8192
Outputs:
- moved: float32 [8192, 8192], P(('groups', 'cls'), 'example'), parts along dimension 0
- losses: float32 [2048], P(('groups', 'example')), parts along dimension 0
There are 2 independent parts, one for each index of `groups`. A program takes and returns all parts, laid end to end along the dimension named above; each array names one. Nothing has to cross between parts.
Inputs may be any that keep to these rules, and one draw needn't show every extreme that they name: `counts`: each block has at least 16 valid slots; some block is full in every draw.
All inputs are finite; a program needn't handle non-finite values.
Results may differ from a plain program's by a relative error of at most 0.006.
Values may be sent and summed in bfloat16 or wider, within the bound.
A program may use at most 128 MiB of HBM per device.

v0:
```python
import jax
import jax.numpy as jnp
from jax import lax
from jax.sharding import PartitionSpec as P

FEATURES = 4096
CLASSES = 8192
ITERS = 2
NEGATIVE = -1e30
LEARNING_RATE = 2e-05
DAMPING_SHARE = 0.1
EPSILON = 1e-06


def body(features, weights, labels, counts, active):
    gathered, labels_all, counts_all = (
        lax.all_gather(features, "example", axis=0, tiled=True),
        lax.all_gather(labels, "example", axis=0, tiled=True),
        lax.all_gather(counts, "example", axis=0, tiled=True),
    )
    all_rows = gathered.shape[0]
    per_device = features.shape[0]
    local_classes = weights.shape[1]
    row_index = jnp.arange(all_rows)
    owner = row_index // per_device
    blocks = jnp.arange(counts_all.shape[0])
    row_limit = jnp.sum(
        jnp.where(owner[:, None] == blocks[None, :], counts_all[None, :], 0), axis=1
    )
    is_valid = (row_index % per_device < row_limit).astype(jnp.float32)
    valid_total = jnp.sum(counts_all).astype(jnp.float32)
    active_count = active[0]
    class_index = lax.axis_index("example") * local_classes + jnp.arange(local_classes)
    is_active = class_index < active_count
    target = (labels_all % active_count).astype(jnp.int32)
    squares = gathered * gathered
    current = weights
    moved = jnp.zeros_like(weights)
    denominator = None
    losses_all = None
    for iteration in range(ITERS):
        current_low = current.astype(jnp.bfloat16)
        logits = lax.psum_scatter(
            jnp.dot(gathered, current_low, preferred_element_type=jnp.float32),
            "cls",
            scatter_dimension=0,
            tiled=True,
        )
        row_start = lax.axis_index("cls") * logits.shape[0]
        row_number = logits.shape[0]
        row_valid = lax.dynamic_slice_in_dim(is_valid, row_start, row_number, 0)
        row_target = lax.dynamic_slice_in_dim(target, row_start, row_number, 0)
        is_label = class_index[None, :] == row_target[:, None]
        masked = jnp.where(is_active[None, :], logits, NEGATIVE)
        local_peak = jnp.max(masked, axis=1)
        local_label = jnp.sum(jnp.where(is_label, logits, 0.0), axis=1)
        row_peak = lax.pmax(local_peak, "example")
        exponent = jnp.exp(masked - row_peak[:, None])
        row_total, label_logit = lax.psum((jnp.sum(exponent, axis=1), local_label), "example")
        probability = exponent / row_total[:, None]
        residual = (
            row_valid[:, None] * (probability - is_label.astype(jnp.float32)) / valid_total
        ).astype(jnp.bfloat16)
        losses_all = row_valid * (row_peak + jnp.log(row_total) - label_logit)
        fisher_weight = None
        if iteration == 0:
            fisher_weight = (
                row_valid[:, None] * probability * (1.0 - probability) / valid_total
            ).astype(jnp.bfloat16)
        if iteration == 0:
            residual, fisher_weight, losses_all = (
                lax.all_gather(residual, "cls", axis=0, tiled=True),
                lax.all_gather(fisher_weight, "cls", axis=0, tiled=True),
                lax.all_gather(losses_all.astype(jnp.bfloat16), "cls", axis=0, tiled=True).astype(
                    losses_all.dtype
                ),
            )
        else:
            residual, losses_all = (
                lax.all_gather(residual, "cls", axis=0, tiled=True),
                lax.all_gather(losses_all.astype(jnp.bfloat16), "cls", axis=0, tiled=True).astype(
                    losses_all.dtype
                ),
            )
        gradient = lax.dot_general(
            gathered, residual, (((0,), (0,)), ((), ())), preferred_element_type=jnp.float32
        )
        if iteration == 0:
            fisher = lax.dot_general(
                squares, fisher_weight, (((0,), (0,)), ((), ())), preferred_element_type=jnp.float32
            )
            fisher_sum = lax.psum(jnp.sum(fisher), ("example", "cls"))
            damping = DAMPING_SHARE * fisher_sum / (FEATURES * CLASSES) + EPSILON
            denominator = fisher + damping
        change = gradient / denominator
        current = current - LEARNING_RATE * change
        moved = moved - change
    own_losses = lax.dynamic_slice_in_dim(
        losses_all, lax.axis_index("example") * per_device, per_device, 0
    )
    return (moved, own_losses)


def solution(mesh):
    return jax.shard_map(
        body,
        mesh=mesh,
        in_specs=(
            P(("groups", "example"), "cls"),
            P(("groups", "cls"), "example"),
            P(("groups", "example")),
            P(("groups", "example")),
            P("groups"),
        ),
        out_specs=(P(("groups", "cls"), "example"), P(("groups", "example"))),
        check_vma=False,
    )
```

profile of v0, /device:TPU:0, one launch (start us, length us, event | category | flops | bytes accessed | tf_op | source)
XLA Modules:
  0.0 353.1 jit_solution(9420997783361034570)
XLA Ops:
  7.2 0.0 all-gather.7.cloned.1.call-start
  7.2 0.7 all-gather.7.cloned.1.call-update
  7.9 0.0 reduce-scatter.3.cloned.1.call-start
  7.9 77.7 %all-gather.7.cloned.1.call-done = bf16[1024,2048]{1,0:T(8,128)(2,1)} async-done(((bf16[128,2048]{1,0:T(8,128)(2,1)}), bf16[1024,2048]{1,0:T(8,128)(2,1)}) %all-gather.7.cloned.1.call-update) | async-done | bytes 4194320 | tf_op jit(solution)/shard_map/all_gather | solution.py:17
  85.6 11.2 %fusion.5 = f32[1024,1024]{1,0:T(8,128)} fusion(bf16[1024,2048]{1,0:T(8,128)(2,1)} %all-gather.7.cloned.1.call-done, f32[2048,1024]{1,0:T(8,128)} %param.6), kind=kOutput, calls=%fused_computation.8 | convolution fusion | flops 4297064448 | bytes 16777216 | tf_op jit(solution)/shard_map/dot_general | solution.py:44
  96.8 0.0 copy-start.4
  96.8 0.0 copy-start.2
  96.8 0.0 reduce-scatter.3.cloned.1.call-update
  96.8 0.0 all-gather.11.cloned.1.call-start
  97.5 0.0 copy-done.4
  97.5 0.6 dynamic-slice
  98.1 0.8 dynamic-update-slice
  98.9 9.9 %all-reduce = s32[8]{0:T(128)S(1)} all-reduce(s32[8]{0:T(128)S(1)} %dynamic-update-slice), channel_id=1, replica_groups=mesh['groups'=2,'example'=8,'cls'=2] {'example'}, use_global_device_ids=true, to_apply=%add | all-reduce | flops 8 | bytes 64
  109.4 0.6 reduce_sum.56
  110.7 0.0 copy-done.2
  110.7 18.2 %all-gather = s32[8,1,128]{2,1,0:T(1,128)S(1)} all-gather(s32[1,1,128]{2,1,0:T(1,128)S(1)} %bitcast.28), channel_id=1, replica_groups=mesh['groups'=2,'example'=8,'cls'=2] {'example'}, dimensions={0}, use_global_device_ids=true | all-gather | bytes 4608 | tf_op jit(solution)/shard_map/all_gather | solution.py:18
  128.9 0.1 broadcast_remainder_fusion
  129.1 0.1 dynamic_slice.12
  129.2 0.1 select_reduce_fusion.2
  129.3 0.1 dynamic_slice.11
  129.3 0.0 reduce-scatter.3.cloned.1.call-done
  129.4 0.0 copy-start
  129.4 2.0 select_reduce_fusion.1
  131.4 17.2 %pmax.14 = f32[512]{0:T(512)S(1)} all-reduce(f32[512]{0:T(512)S(1)} %select_reduce_fusion.1), channel_id=1, replica_groups=mesh['groups'=2,'example'=8,'cls'=2] {'example'}, use_global_device_ids=true, to_apply=%region_3.4 | all-reduce | flops 512 | bytes 4096 | tf_op jit(solution)/shard_map/pmax | solution.py:57
  148.6 0.0 copy-done
  148.6 0.5 fusion.16
  149.1 19.1 %psum.28 = f32[512]{0:T(512)S(1)} all-reduce(f32[512]{0:T(512)S(1)} %fusion.16), channel_id=1, replica_groups=mesh['groups'=2,'example'=8,'cls'=2] {'example'}, use_global_device_ids=true, to_apply=%region_5.6 | all-reduce | flops 512 | bytes 4096 | tf_op jit(solution)/shard_map/psum | solution.py:59
  168.1 2.8 fusion.13
  170.9 0.0 all-gather.11.cloned.1.call-update
  170.9 0.0 all-gather.9.cloned.1.call-start
  171.0 0.5 all-gather.9.cloned.1.call-update
  171.5 0.0 reduce-scatter.5.cloned.1.call-start
  171.6 9.2 %copy.16 = f32[2048,1024]{0,1:T(8,128)} copy(f32[2048,1024]{1,0:T(8,128)} %param.6) | data formatting | bytes 16777216 | tf_op args[1]
  180.8 0.0 all-gather.11.cloned.1.call-done
  180.8 11.4 %fusion.26 = (f32[]{:T(128)}, f32[2048,1024]{1,0:T(8,128)}) fusion(bf16[1024,1024]{1,0:T(8,128)(2,1)} %all-gather.11.cloned.1.call-done, bf16[1024,2048]{1,0:T(8,128)(2,1)} %all-gather.7.cloned.1.call-done), kind=kOutput, calls=%fused_computation.49 | convolution fusion | flops 4299161600 | bytes 14680068 | tf_op jit(solution)/shard_map/dot_general | solution.py:89
  192.2 33.1 %psum.29 = f32[]{:T(128)} all-reduce(f32[]{:T(128)} %get-tuple-element.14), channel_id=1, replica_groups=mesh['groups'=2,'example'=8,'cls'=2] {'example','cls'}, use_global_device_ids=true, to_apply=%region_8.9 | all-reduce | flops 1 | bytes 8 | tf_op jit(solution)/shard_map/psum | solution.py:92
  225.4 9.1 %copy.15 = f32[2048,1024]{0,1:T(8,128)} copy(f32[2048,1024]{1,0:T(8,128)} %get-tuple-element.15) | data formatting | bytes 16777216 | tf_op jit(solution)/shard_map/dot_general | solution.py:89
  235.1 0.0 all-gather.9.cloned.1.call-done
  235.2 0.0 copy-start.3
  235.2 10.1 %bitcast_divide_fusion.1 = f32[2048,1024]{0,1:T(8,128)S(1)} fusion(f32[2048,1024]{0,1:T(8,128)} %copy.15, bf16[1024,1024]{1,0:T(8,128)(2,1)} %all-gather.9.cloned.1.call-done, bf16[1024,2048]{1,0:T(8,128)(2,1)} %all-gather.7.cloned.1.call-done, f32[]{:T(128)S(6)} %add.68), kind=kOutput, calls=%fused_computation.2 | convolution fusion | flops 4299161600 | bytes 23068676 | tf_op jit(solution)/shard_map/dot_general | solution.py:85
  245.3 0.0 copy-start.5
  245.3 3.4 copy-done.5
  248.7 0.0 copy-done.3
  248.7 9.5 %fusion.7 = f32[1024,1024]{1,0:T(8,128)} fusion(bf16[1024,2048]{1,0:T(8,128)(2,1)S(1)} %copy-done.3, f32[2048,1024]{0,1:T(8,128)} %copy.16, f32[2048,1024]{0,1:T(8,128)S(1)} %bitcast_divide_fusion.1), kind=kOutput, calls=%fused_computation.13 | convolution fusion | flops 4301258752 | bytes 25165824 | tf_op jit(solution)/shard_map/dot_general | solution.py:44
  258.2 0.0 reduce-scatter.5.cloned.1.call-update
  258.3 0.0 all-gather.13.cloned.1.call-start
  258.3 9.4 %reduce-scatter.5.cloned.1.call-done = f32[512,1024]{1,0:T(8,128)} async-done(((f32[1024,1024]{1,0:T(8,128)}), f32[512,1024]{1,0:T(8,128)}) %reduce-scatter.5.cloned.1.call-update) | async-done | bytes 2097168 | tf_op jit(solution)/shard_map/reduce_scatter | solution.py:43
  267.7 0.0 copy-start.1
  267.7 2.0 select_reduce_fusion
  269.7 21.7 %pmax.15 = f32[512]{0:T(512)S(1)} all-reduce(f32[512]{0:T(512)S(1)} %select_reduce_fusion), channel_id=1, replica_groups=mesh['groups'=2,'example'=8,'cls'=2] {'example'}, use_global_device_ids=true, to_apply=%region_11.12 | all-reduce | flops 512 | bytes 4096 | tf_op jit(solution)/shard_map/pmax | solution.py:57
  291.4 0.0 copy-done.1
  291.4 0.7 fusion.8
  292.2 17.2 %all-reduce.1 = (f32[512]{0:T(512)S(1)}, f32[512]{0:T(512)S(1)}) all-reduce(f32[512]{0:T(512)S(1)} %get-tuple-element.9, f32[512]{0:T(512)S(1)} %get-tuple-element.8), channel_id=1, replica_groups=mesh['groups'=2,'example'=8,'cls'=2] {'example'}, use_global_device_ids=true, to_apply=%region_13.14 | all-reduce | flops 1024 | bytes 8192 | tf_op jit(solution)/shard_map/psum | solution.py:59
  309.3 2.1 fusion.14
  311.5 0.0 all-gather.13.cloned.1.call-update
  311.5 0.1 multiply_convert_fusion
  311.6 2.0 all-gather.1
  313.6 0.6 dynamic_slice.13
  314.2 6.6 %all-gather.13.cloned.1.call-done = bf16[1024,1024]{1,0:T(8,128)(2,1)} async-done(((bf16[512,1024]{1,0:T(8,128)(2,1)}), bf16[1024,1024]{1,0:T(8,128)(2,1)}) %all-gather.13.cloned.1.call-update) | async-done | bytes 2097168 | tf_op jit(solution)/shard_map/all_gather | solution.py:80
  320.9 16.2 %fusion = f32[2048,1024]{0,1:T(8,128)} fusion(f32[2048,1024]{0,1:T(8,128)} %copy-done.5, f32[2048,1024]{0,1:T(8,128)} %copy.15, bf16[1024,1024]{1,0:T(8,128)(2,1)} %all-gather.13.cloned.1.call-done, bf16[1024,2048]{1,0:T(8,128)(2,1)} %all-gather.7.cloned.1.call-done, f32[]{:T(128)S(6)} %add.68), kind=kOutput, calls=%fused_computation.1 | convolution fusion | flops 4303355904 | bytes 31457284 | tf_op jit(solution)/shard_map/dot_general | solution.py:85
  337.1 9.2 %copy.18 = f32[2048,1024]{1,0:T(8,128)} copy(f32[2048,1024]{0,1:T(8,128)} %fusion) | data formatting | bytes 16777216
  (8 shorter events, 0.0 us)
Async XLA Ops:
  7.2 78.5 %all-gather.7.cloned.1.call-start = ((), (), s32[]{:S(2)}) async-start(), calls=%async_computation.2 | async-start | bytes 4718592 | tf_op jit(solution)/shard_map/all_gather | solution.py:17
  7.9 121.5 %reduce-scatter.3.cloned.1.call-start = ((), (), s32[]{:S(2)}) async-start(), calls=%async_computation.3 | async-start | bytes 6291456 | tf_op jit(solution)/shard_map/reduce_scatter | solution.py:43
  96.8 0.7 copy-start.4
  96.8 13.9 %copy-start.2 = (s32[128]{0:T(128)S(1)}, s32[128]{0:T(128)}, u32[]{:S(2)}) copy-start(s32[128]{0:T(128)} %param.7) | copy-start | bytes 1540
  96.8 84.0 %all-gather.11.cloned.1.call-start = ((), (), s32[]{:S(2)}) async-start(), calls=%async_computation.5 | async-start | bytes 3145728 | tf_op jit(solution)/shard_map/all_gather | solution.py:73
  129.4 19.2 %copy-start = (f32[512,1024]{1,0:T(8,128)S(1)}, f32[512,1024]{1,0:T(8,128)}, u32[]{:S(2)}) copy-start(f32[512,1024]{1,0:T(8,128)} %reduce-scatter.3.cloned.1.call-done) | copy-start | bytes 6291460
  170.9 64.2 %all-gather.9.cloned.1.call-start = ((), (), s32[]{:S(2)}) async-start(), calls=%async_computation.4 | async-start | bytes 3145728 | tf_op jit(solution)/shard_map/all_gather | solution.py:72
  171.5 96.2 %reduce-scatter.5.cloned.1.call-start = ((), (), s32[]{:S(2)}) async-start(), calls=%async_computation.6 | async-start | bytes 6291456 | tf_op jit(solution)/shard_map/reduce_scatter | solution.py:43
  235.2 13.5 %copy-start.3 = (bf16[1024,2048]{1,0:T(8,128)(2,1)S(1)}, bf16[1024,2048]{1,0:T(8,128)(2,1)}, u32[]{:S(2)}) copy-start(bf16[1024,2048]{1,0:T(8,128)(2,1)} %all-gather.7.cloned.1.call-done) | copy-start | bytes 12582916
  245.3 3.4 copy-start.5
  258.3 62.6 %all-gather.13.cloned.1.call-start = ((), (), s32[]{:S(2)}) async-start(), calls=%async_computation.7 | async-start | bytes 3145728 | tf_op jit(solution)/shard_map/all_gather | solution.py:80
  267.7 23.7 %copy-start.1 = (f32[512,1024]{1,0:T(8,128)S(1)}, f32[512,1024]{1,0:T(8,128)}, u32[]{:S(2)}) copy-start(f32[512,1024]{1,0:T(8,128)} %reduce-scatter.5.cloned.1.call-done) | copy-start | bytes 6291460
Sparse Core Ops, SparseCore 0:
  10.1 75.5 all-gather.6
  97.0 10.5 reduce-scatter.2
  171.1 7.7 all-gather.10
  180.3 11.7 all-gather.8
  258.4 9.2 reduce-scatter.4
  311.6 9.2 all-gather.12
where the time goes:
time: 354 us; the launch traced here: 353 us
  blocking collectives  138 us (39%)
  waiting for transfers between devices  95 us (27%)
  matrix products  58.4 us (16%)
  local copies, waits for them, and re-layouts  33.1 us (9%)
  between operations  16.8 us (5%)
  other arithmetic  11.1 us (3%)
    all_gather x1, waiting for transfers between devices, body(): lax.all_gather(features, 'example', axis=0, tiled=True)  77.7 us
    pmax x2, blocking collectives, body(): row_peak = lax.pmax(local_peak, 'example')  38.9 us
    psum x2, blocking collectives, body(): lax.psum((jnp.sum(exponent, axis=1), local_label), 'example')  36.3 us
    psum x1, blocking collectives, body(): fisher_sum = lax.psum(jnp.sum(fisher), ('example', 'cls'))  33.1 us
    dot_general x2, matrix products, body(): lax.dot_general(gathered, residual, (((0,), (0,)), ((), ())), preferred_e...  26.3 us
    unnamed x18, local copies, waits for them, and re-layouts  23.2 us
    dot_general x2, matrix products, body(): jnp.dot(gathered, current_low, preferred_element_type=jnp.float32)  20.7 us
    all_gather x1, blocking collectives, body(): lax.all_gather(labels, 'example', axis=0, tiled=True)  18.2 us
  transfers between devices with their start and end apart: 6, of which 3 were waited for; matrix products, arithmetic and copies ran while one was open for 9% of the time, Pallas kernels for 0%

commit v1 on v0

--- a/solution.py
+++ b/solution.py
@@ -12,9 +12,39 @@
 EPSILON = 1e-06
 
 
+def _advance_desk(vector, at_axis):
+    vector = jnp.moveaxis(vector, 0, at_axis)
+    piece_next = vector.shape
+    return vector.reshape(
+        *piece_next[:at_axis],
+        piece_next[at_axis] * piece_next[at_axis + 1],
+        *piece_next[at_axis + 2 :]
+    )
+
+
 def body(features, weights, labels, counts, active):
+
+    def tasks_render(packet, mesh_name, dim_k):
+        shares = jax.lax.psum(1, mesh_name)
+        copies = list(map(lambda c: (c, (c + 1) % shares), range(shares)))
+        so_far_all = [(s, rr) for rr, s in copies]
+        value_now, met_up = ([], [])
+        for i0 in range(shares - 1):
+            if i0 % 2 == 0:
+                shaped = jax.lax.ppermute(value_now[-1] if value_now else packet, mesh_name, copies)
+                value_now.append(shaped)
+            else:
+                v_next = jax.lax.ppermute(met_up[-1] if met_up else packet, mesh_name, so_far_all)
+                met_up.append(v_next)
+        prior = jnp.stack([*value_now[::-1], packet, *met_up])
+        h_now = len(value_now)
+        mid_arr = jax.lax.axis_index(mesh_name)
+        val = mid_arr - h_now
+        prior = prior[(jnp.arange(shares) - val) % shares]
+        return _advance_desk(prior, dim_k)
+
     gathered, labels_all, counts_all = (
-        lax.all_gather(features, "example", axis=0, tiled=True),
+        tasks_render(features, "example", 0),
         lax.all_gather(labels, "example", axis=0, tiled=True),
         lax.all_gather(counts, "example", axis=0, tiled=True),
     )

time: 354 us -> 362 us (1.023)
  starting transfers between devices: 0.24 us -> 39.2 us
  waiting for transfers between devices: 95 us -> 72.7 us
  local copies, waits for them, and re-layouts: 33.1 us -> 18 us
  blocking collectives: 138 us -> 142 us
    all_gather x1 -> x0, waiting for transfers between devices: 77.7 us -> none  [body(): lax.all_gather(features, 'example', axis=0, tiled=True)]
    ppermute x0 -> x7, waiting for transfers between devices: none -> 49.5 us  [the longest x4 49.5 us: tasks_render(): jax.lax.ppermute(value_now[-1] if value_now else packet, mesh_name, copies)]
    ppermute x0 -> x7, starting transfers between devices: none -> 38.6 us  [the longest x3 30.6 us: tasks_render(): jax.lax.ppermute(met_up[-1] if met_up else packet, mesh_name, so_far_all)]
    unnamed x18 -> x25, local copies, waits for them, and re-layouts: 23.2 us -> 11.4 us
    dot_general x1 -> x0, local copies, waits for them, and re-layouts: 9.14 us -> none  [body(): lax.dot_general(squares, fisher_weight, (((0,), (0,)), ((), ())), preferr...]
    all_gather x1, waiting for transfers between devices: 0.01 us -> 6.36 us  [body(): lax.all_gather(fisher_weight, 'cls', axis=0, tiled=True)]
    gather x0 -> x1, local copies, waits for them, and re-layouts: none -> 4.98 us  [tasks_render(): prior = prior[(jnp.arange(shares) - val) % shares]]
    all_gather x1, blocking collectives: 18.2 us -> 22.7 us  [body(): lax.all_gather(labels, 'example', axis=0, tiled=True)]
  transfers between devices with their start and end apart: 6 -> 12, of which waited for: 3 -> 7; matrix products, arithmetic and copies ran while one was open for 9% -> 6% of each run, Pallas kernels for 0% -> 0%
where the time goes in v1:
time: 362 us; the launch traced here: 361 us
  blocking collectives  142 us (39%)
  waiting for transfers between devices  72.7 us (20%)
  matrix products  58.7 us (16%)
  starting transfers between devices  39.2 us (11%)
  local copies, waits for them, and re-layouts  18 us (5%)
  between operations  16.5 us (5%)
  other arithmetic  14.3 us (4%)
    ppermute x4, waiting for transfers between devices, tasks_render(): jax.lax.ppermute(value_now[-1] if value_now else packet, mesh_name, copies)  49.5 us
    pmax x2, blocking collectives, body(): row_peak = lax.pmax(local_peak, 'example')  38.9 us
    psum x2, blocking collectives, body(): lax.psum((jnp.sum(exponent, axis=1), local_label), 'example')  36.3 us
    psum x1, blocking collectives, body(): fisher_sum = lax.psum(jnp.sum(fisher), ('example', 'cls'))  34.5 us
    ppermute x3, starting transfers between devices, tasks_render(): jax.lax.ppermute(met_up[-1] if met_up else packet, mesh_name, so_far_all)  30.6 us
    dot_general x2, matrix products, body(): lax.dot_general(gathered, residual, (((0,), (0,)), ((), ())), preferred_e...  26.5 us
    all_gather x1, blocking collectives, body(): lax.all_gather(labels, 'example', axis=0, tiled=True)  22.7 us
    dot_general x2, matrix products, body(): jnp.dot(gathered, current_low, preferred_element_type=jnp.float32)  20.6 us
  transfers between devices with their start and end apart: 12, of which 7 were waited for; matrix products, arithmetic and copies ran while one was open for 6% of the time, Pallas kernels for 0%

profile of v1, /device:TPU:0, one launch (start us, length us, event | category | flops | bytes accessed | tf_op | source)
XLA Modules:
  0.0 361.0 jit_solution(9159252250459676846)
XLA Ops:
  7.2 0.0 reduce-scatter.3.cloned.1.call-start
  7.2 3.0 collective-permute-start
  10.3 15.2 %collective-permute-done = bf16[128,2048]{1,0:T(8,128)(2,1)S(1)} collective-permute-done((bf16[128,2048]{1,0:T(8,128)(2,1)}, bf16[128,2048]{1,0:T(8,128)(2,1)S(1)}, u32[]{:S(2)}, u32[]{:S(2)}) %collective-permute-start) | collective-permute-done | bytes 524320 | tf_op jit(solution)/shard_map/ppermute | solution.py:34
  25.4 4.7 %collective-permute-start.4 = (bf16[128,2048]{1,0:T(8,128)(2,1)}, bf16[128,2048]{1,0:T(8,128)(2,1)S(1)}, u32[]{:S(2)}, u32[]{:S(2)}) collective-permute-start(bf16[128,2048]{1,0:T(8,128)(2,1)} %param.5), channel_id=1, source_target_pairs={{2,0},{4,2},{6,4},{8,6},{10,8},{12,10},{14,12},{0,14},{3,1},{5,3},... | collective-permute-start | bytes 1572872 | tf_op jit(solution)/shard_map/ppermute | solution.py:37
  30.2 17.4 %collective-permute-done.1 = bf16[128,2048]{1,0:T(8,128)(2,1)S(1)} collective-permute-done((bf16[128,2048]{1,0:T(8,128)(2,1)S(1)}, bf16[128,2048]{1,0:T(8,128)(2,1)S(1)}, u32[]{:S(2)}, u32[]{:S(2)}) %collective-permute-start.1) | collective-permute-done | bytes 524320 | tf_op jit(solution)/shard_map/ppermute | solution.py:34
  47.6 2.5 collective-permute-start.2
  50.0 12.3 %collective-permute-start.5 = (bf16[128,2048]{1,0:T(8,128)(2,1)S(1)}, bf16[128,2048]{1,0:T(8,128)(2,1)S(1)}, u32[]{:S(2)}, u32[]{:S(2)}) collective-permute-start(bf16[128,2048]{1,0:T(8,128)(2,1)S(1)} %collective-permute-done.4), channel_id=1, source_target_pairs={{2,0},{4,2},{6,4},{8,6},{10,8},{12,10},{14,12},{0,14},{3,1},{5,3},... | collective-permute-start | bytes 1572872 | tf_op jit(solution)/shard_map/ppermute | solution.py:37
  62.4 8.9 %collective-permute-done.2 = bf16[128,2048]{1,0:T(8,128)(2,1)S(1)} collective-permute-done((bf16[128,2048]{1,0:T(8,128)(2,1)S(1)}, bf16[128,2048]{1,0:T(8,128)(2,1)S(1)}, u32[]{:S(2)}, u32[]{:S(2)}) %collective-permute-start.2) | collective-permute-done | bytes 524320 | tf_op jit(solution)/shard_map/ppermute | solution.py:34
  71.3 2.5 collective-permute-start.3
  73.8 0.0 collective-permute-done.5
  73.8 13.5 %collective-permute-start.6 = (bf16[128,2048]{1,0:T(8,128)(2,1)S(1)}, bf16[128,2048]{1,0:T(8,128)(2,1)S(1)}, u32[]{:S(2)}, u32[]{:S(2)}) collective-permute-start(bf16[128,2048]{1,0:T(8,128)(2,1)S(1)} %collective-permute-done.5), channel_id=1, source_target_pairs={{2,0},{4,2},{6,4},{8,6},{10,8},{12,10},{14,12},{0,14},{3,1},{5,3},... | collective-permute-start | bytes 1572872 | tf_op jit(solution)/shard_map/ppermute | solution.py:37
  87.4 8.0 %collective-permute-done.3 = bf16[128,2048]{1,0:T(8,128)(2,1)} collective-permute-done((bf16[128,2048]{1,0:T(8,128)(2,1)S(1)}, bf16[128,2048]{1,0:T(8,128)(2,1)}, u32[]{:S(2)}, u32[]{:S(2)}) %collective-permute-start.3) | collective-permute-done | bytes 524320 | tf_op jit(solution)/shard_map/ppermute | solution.py:34
  95.4 1.9 bitcast_dynamic-update-slice_fusion.7
  97.2 0.8 bitcast_dynamic-update-slice_fusion.6
  98.1 0.8 bitcast_dynamic-update-slice_fusion.5
  98.9 0.8 bitcast_dynamic-update-slice_fusion.4
  99.7 0.8 bitcast_dynamic-update-slice_fusion.3
  100.6 0.8 bitcast_dynamic-update-slice_fusion.2
  101.4 0.8 bitcast_dynamic-update-slice_fusion.1
  102.2 0.8 bitcast_dynamic-update-slice_fusion
  103.1 5.0 %gather_fusion = bf16[8,128,2048]{2,1,0:T(8,128)(2,1)} fusion(bf16[8,128,2048]{2,1,0:T(8,128)(2,1)} %bitcast_dynamic-update-slice_fusion, s32[1024]{0:T(1024)S(1)} %pad_clamp_fusion), kind=kCustom, calls=%fused_computation | custom fusion | bytes 8388640 | tf_op jit(solution)/shard_map/gather | solution.py:43
  108.0 11.2 %fusion.4 = f32[1024,1024]{1,0:T(8,128)} fusion(bf16[1024,2048]{1,0:T(8,128)(2,1)} %bitcast.36, f32[2048,1024]{1,0:T(8,128)} %param.6), kind=kOutput, calls=%fused_computation.8 | convolution fusion | flops 4297064448 | bytes 16777216 | tf_op jit(solution)/shard_map/dot_general | solution.py:74
  119.2 0.0 reduce-scatter.3.cloned.1.call-update
  119.2 0.0 all-gather.8.cloned.1.call-start
  119.9 0.6 dynamic-slice
  120.5 0.8 dynamic-update-slice
  121.3 7.4 %all-reduce = s32[8]{0:T(128)S(1)} all-reduce(s32[8]{0:T(128)S(1)} %dynamic-update-slice), channel_id=1, replica_groups=mesh['groups'=2,'example'=8,'cls'=2] {'example'}, use_global_device_ids=true, to_apply=%add | all-reduce | flops 8 | bytes 64
  129.3 0.6 reduce_sum.56
  130.6 22.7 %all-gather = s32[8,1,128]{2,1,0:T(1,128)S(1)} all-gather(s32[1,1,128]{2,1,0:T(1,128)S(1)} %bitcast.44), channel_id=1, replica_groups=mesh['groups'=2,'example'=8,'cls'=2] {'example'}, dimensions={0}, use_global_device_ids=true | all-gather | bytes 4608 | tf_op jit(solution)/shard_map/all_gather | solution.py:48
  153.4 0.1 broadcast_remainder_fusion
  153.5 0.1 dynamic_slice.12
  153.6 0.1 select_reduce_fusion.2
  153.7 0.1 dynamic_slice.11
  153.8 0.0 reduce-scatter.3.cloned.1.call-done
  153.8 2.0 select_reduce_fusion.1
  155.8 17.1 %pmax.14 = f32[512]{0:T(512)S(1)} all-reduce(f32[512]{0:T(512)S(1)} %select_reduce_fusion.1), channel_id=1, replica_groups=mesh['groups'=2,'example'=8,'cls'=2] {'example'}, use_global_device_ids=true, to_apply=%region_3.4 | all-reduce | flops 512 | bytes 4096 | tf_op jit(solution)/shard_map/pmax | solution.py:87
  172.9 2.1 fusion.14
  175.0 19.1 %psum.28 = f32[512]{0:T(512)S(1)} all-reduce(f32[512]{0:T(512)S(1)} %fusion.14), channel_id=1, replica_groups=mesh['groups'=2,'example'=8,'cls'=2] {'example'}, use_global_device_ids=true, to_apply=%region_5.6 | all-reduce | flops 512 | bytes 4096 | tf_op jit(solution)/shard_map/psum | solution.py:89
  194.1 2.8 fusion.11
  196.9 0.0 all-gather.8.cloned.1.call-update
  196.9 0.0 all-gather.6.cloned.1.call-start
  197.0 0.7 all-gather.6.cloned.1.call-update
  197.7 0.2 reduce-scatter.5.cloned.1.call-start
  197.9 6.4 %all-gather.8.cloned.1.call-done = bf16[1024,1024]{1,0:T(8,128)(2,1)} async-done(((bf16[512,1024]{1,0:T(8,128)(2,1)}), bf16[1024,1024]{1,0:T(8,128)(2,1)}) %all-gather.8.cloned.1.call-update) | async-done | bytes 2097168 | tf_op jit(solution)/shard_map/all_gather | solution.py:103
  204.3 11.7 %fusion.26 = (f32[]{:T(128)}, f32[2048,1024]{1,0:T(8,128)}) fusion(bf16[1024,1024]{1,0:T(8,128)(2,1)} %all-gather.8.cloned.1.call-done, bf16[1024,2048]{1,0:T(8,128)(2,1)} %bitcast.37), kind=kOutput, calls=%fused_computation.63 | convolution fusion | flops 4299161600 | bytes 14680068 | tf_op jit(solution)/shard_map/dot_general | solution.py:119
  215.9 34.5 %psum.29 = f32[]{:T(128)} all-reduce(f32[]{:T(128)} %get-tuple-element.8), channel_id=1, replica_groups=mesh['groups'=2,'example'=8,'cls'=2] {'example','cls'}, use_global_device_ids=true, to_apply=%region_8.9 | all-reduce | flops 1 | bytes 8 | tf_op jit(solution)/shard_map/psum | solution.py:122
  251.1 0.0 all-gather.6.cloned.1.call-done
  251.1 10.1 %add_divide_fusion = f32[2048,1024]{1,0:T(8,128)S(1)} fusion(f32[2048,1024]{1,0:T(8,128)} %get-tuple-element.9, f32[]{:T(128)S(6)} %add.94, bf16[1024,2048]{1,0:T(8,128)(2,1)} %bitcast.38, bf16[1024,1024]{1,0:T(8,128)(2,1)} %all-gather.6.cloned.1.call-done), kind=kOutput, calls=%fused_computation.3 | convolution fusion | flops 4299161600 | bytes 23068676 | tf_op jit(solution)/shard_map/dot_general | solution.py:115
  261.3 3.2 copy-done.6
  264.5 9.4 %fusion = f32[1024,1024]{1,0:T(8,128)} fusion(bf16[1024,2048]{1,0:T(8,128)(2,1)S(1)} %bitcast.40, f32[2048,1024]{1,0:T(8,128)} %param.6, f32[2048,1024]{1,0:T(8,128)S(1)} %add_divide_fusion), kind=kOutput, calls=%fused_computation.4 | convolution fusion | flops 4301258752 | bytes 25165824 | tf_op jit(solution)/shard_map/dot_general | solution.py:74
  273.9 0.0 reduce-scatter.5.cloned.1.call-update
  273.9 0.3 all-gather.10.cloned.1.call-start
  274.2 9.2 %reduce-scatter.5.cloned.1.call-done = f32[512,1024]{1,0:T(8,128)} async-done(((f32[1024,1024]{1,0:T(8,128)}), f32[512,1024]{1,0:T(8,128)}) %reduce-scatter.5.cloned.1.call-update) | async-done | bytes 2097168 | tf_op jit(solution)/shard_map/reduce_scatter | solution.py:73
  283.4 2.0 select_reduce_fusion
  285.4 21.8 %pmax.15 = f32[512]{0:T(512)S(1)} all-reduce(f32[512]{0:T(512)S(1)} %select_reduce_fusion), channel_id=1, replica_groups=mesh['groups'=2,'example'=8,'cls'=2] {'example'}, use_global_device_ids=true, to_apply=%region_11.12 | all-reduce | flops 512 | bytes 4096 | tf_op jit(solution)/shard_map/pmax | solution.py:87
  307.1 2.3 fusion.6
  309.4 17.2 %all-reduce.1 = (f32[512]{0:T(512)S(1)}, f32[512]{0:T(512)S(1)}) all-reduce(f32[512]{0:T(512)S(1)} %get-tuple-element.3, f32[512]{0:T(512)S(1)} %get-tuple-element.2), channel_id=1, replica_groups=mesh['groups'=2,'example'=8,'cls'=2] {'example'}, use_global_device_ids=true, to_apply=%region_13.14 | all-reduce | flops 1024 | bytes 8192 | tf_op jit(solution)/shard_map/psum | solution.py:89
  326.6 2.2 fusion.12
  328.8 0.0 all-gather.10.cloned.1.call-update
  328.8 0.1 multiply_convert_fusion
  328.9 1.8 all-gather.1
  330.7 0.6 dynamic_slice.13
  331.3 6.9 %all-gather.10.cloned.1.call-done = bf16[1024,1024]{1,0:T(8,128)(2,1)} async-done(((bf16[512,1024]{1,0:T(8,128)(2,1)}), bf16[1024,1024]{1,0:T(8,128)(2,1)}) %all-gather.10.cloned.1.call-update) | async-done | bytes 2097168 | tf_op jit(solution)/shard_map/all_gather | solution.py:110
  338.1 16.4 %divide_subtract_fusion = f32[2048,1024]{1,0:T(8,128)} fusion(f32[2048,1024]{1,0:T(8,128)} %copy-done.6, f32[2048,1024]{1,0:T(8,128)} %get-tuple-element.9, f32[]{:T(128)S(6)} %add.94, bf16[1024,2048]{1,0:T(8,128)(2,1)} %bitcast.39, bf16[1024,1024]{1,0:T(8,128)(2,1)} %all-gather.10.cloned.1.call-done), kind=kOutput, calls=%fused_computation.1 | convolution fusion | flops 4303355904 | bytes 31457284 | tf_op jit(solution)/shard_map/dot_general | solution.py:115
  (26 shorter events, 0.1 us)
Async XLA Ops:
  7.2 92.6 %copy-start.3 = (bf16[128,2048]{1,0:T(8,128)(2,1)S(1)}, bf16[128,2048]{1,0:T(8,128)(2,1)}, u32[]{:S(2)}) copy-start(bf16[128,2048]{1,0:T(8,128)(2,1)} %param.5) | copy-start | bytes 1572868
  7.2 146.6 %reduce-scatter.3.cloned.1.call-start = ((), (), s32[]{:S(2)}) async-start(), calls=%async_computation.2 | async-start | bytes 6291456 | tf_op jit(solution)/shard_map/reduce_scatter | solution.py:73
  7.2 18.2 %collective-permute-start = (bf16[128,2048]{1,0:T(8,128)(2,1)}, bf16[128,2048]{1,0:T(8,128)(2,1)S(1)}, u32[]{:S(2)}, u32[]{:S(2)}) collective-permute-start(bf16[128,2048]{1,0:T(8,128)(2,1)} %param.5), channel_id=1, source_target_pairs={{0,2},{2,4},{4,6},{6,8},{8,10},{10,12},{12,14},{14,0},{1,3},{3,5},... | collective-permute-start | bytes 1572872 | tf_op jit(solution)/shard_map/ppermute | solution.py:34
  25.4 22.1 %collective-permute-start.1 = (bf16[128,2048]{1,0:T(8,128)(2,1)S(1)}, bf16[128,2048]{1,0:T(8,128)(2,1)S(1)}, u32[]{:S(2)}, u32[]{:S(2)}) collective-permute-start(bf16[128,2048]{1,0:T(8,128)(2,1)S(1)} %collective-permute-done), channel_id=1, source_target_pairs={{0,2},{2,4},{4,6},{6,8},{8,10},{10,12},{12,14},{14,0},{1,3},{3,5},... | collective-permute-start | bytes 1572872 | tf_op jit(solution)/shard_map/ppermute | solution.py:34
  25.4 24.6 %collective-permute-start.4 = (bf16[128,2048]{1,0:T(8,128)(2,1)}, bf16[128,2048]{1,0:T(8,128)(2,1)S(1)}, u32[]{:S(2)}, u32[]{:S(2)}) collective-permute-start(bf16[128,2048]{1,0:T(8,128)(2,1)} %param.5), channel_id=1, source_target_pairs={{2,0},{4,2},{6,4},{8,6},{10,8},{12,10},{14,12},{0,14},{3,1},{5,3},... | collective-permute-start | bytes 1572872 | tf_op jit(solution)/shard_map/ppermute | solution.py:37
  47.6 23.8 %collective-permute-start.2 = (bf16[128,2048]{1,0:T(8,128)(2,1)S(1)}, bf16[128,2048]{1,0:T(8,128)(2,1)S(1)}, u32[]{:S(2)}, u32[]{:S(2)}) collective-permute-start(bf16[128,2048]{1,0:T(8,128)(2,1)S(1)} %collective-permute-done.1), channel_id=1, source_target_pairs={{0,2},{2,4},{4,6},{6,8},{8,10},{10,12},{12,14},{14,0},{1,3},{3,5},... | collective-permute-start | bytes 1572872 | tf_op jit(solution)/shard_map/ppermute | solution.py:34
  50.0 23.8 %collective-permute-start.5 = (bf16[128,2048]{1,0:T(8,128)(2,1)S(1)}, bf16[128,2048]{1,0:T(8,128)(2,1)S(1)}, u32[]{:S(2)}, u32[]{:S(2)}) collective-permute-start(bf16[128,2048]{1,0:T(8,128)(2,1)S(1)} %collective-permute-done.4), channel_id=1, source_target_pairs={{2,0},{4,2},{6,4},{8,6},{10,8},{12,10},{14,12},{0,14},{3,1},{5,3},... | collective-permute-start | bytes 1572872 | tf_op jit(solution)/shard_map/ppermute | solution.py:37
  71.3 24.0 %collective-permute-start.3 = (bf16[128,2048]{1,0:T(8,128)(2,1)S(1)}, bf16[128,2048]{1,0:T(8,128)(2,1)}, u32[]{:S(2)}, u32[]{:S(2)}) collective-permute-start(bf16[128,2048]{1,0:T(8,128)(2,1)S(1)} %collective-permute-done.2), channel_id=1, source_target_pairs={{0,2},{2,4},{4,6},{6,8},{8,10},{10,12},{12,14},{14,0},{1,3},{3,5},... | collective-permute-start | bytes 1572872 | tf_op jit(solution)/shard_map/ppermute | solution.py:34
  73.8 28.4 %collective-permute-start.6 = (bf16[128,2048]{1,0:T(8,128)(2,1)S(1)}, bf16[128,2048]{1,0:T(8,128)(2,1)S(1)}, u32[]{:S(2)}, u32[]{:S(2)}) collective-permute-start(bf16[128,2048]{1,0:T(8,128)(2,1)S(1)} %collective-permute-done.5), channel_id=1, source_target_pairs={{2,0},{4,2},{6,4},{8,6},{10,8},{12,10},{14,12},{0,14},{3,1},{5,3},... | collective-permute-start | bytes 1572872 | tf_op jit(solution)/shard_map/ppermute | solution.py:37
  119.2 0.7 copy-start.5
  119.2 11.4 %copy-start.4 = (s32[128]{0:T(128)S(1)}, s32[128]{0:T(128)}, u32[]{:S(2)}) copy-start(s32[128]{0:T(128)} %param.7) | copy-start | bytes 1540
  119.2 85.0 %all-gather.8.cloned.1.call-start = ((), (), s32[]{:S(2)}) async-start(), calls=%async_computation.4 | async-start | bytes 3145728 | tf_op jit(solution)/shard_map/all_gather | solution.py:103
  153.8 40.3 %copy-start = (f32[512,1024]{1,0:T(8,128)S(1)}, f32[512,1024]{1,0:T(8,128)}, u32[]{:S(2)}) copy-start(f32[512,1024]{1,0:T(8,128)} %reduce-scatter.3.cloned.1.call-done) | copy-start | bytes 6291460
  196.9 54.2 %all-gather.6.cloned.1.call-start = ((), (), s32[]{:S(2)}) async-start(), calls=%async_computation.3 | async-start | bytes 3145728 | tf_op jit(solution)/shard_map/all_gather | solution.py:102
  197.7 85.7 %reduce-scatter.5.cloned.1.call-start = ((), (), s32[]{:S(2)}) async-start(), calls=%async_computation.5 | async-start | bytes 6291456 | tf_op jit(solution)/shard_map/reduce_scatter | solution.py:73
  251.1 13.4 %copy-start.2 = (bf16[8,128,2048]{2,1,0:T(8,128)(2,1)S(1)}, bf16[8,128,2048]{2,1,0:T(8,128)(2,1)}, u32[]{:S(2)}) copy-start(bf16[8,128,2048]{2,1,0:T(8,128)(2,1)} %gather_fusion) | copy-start | bytes 12582916
  261.2 3.2 copy-start.6
  273.9 64.2 %all-gather.10.cloned.1.call-start = ((), (), s32[]{:S(2)}) async-start(), calls=%async_computation.6 | async-start | bytes 3145728 | tf_op jit(solution)/shard_map/all_gather | solution.py:110
  283.4 43.2 %copy-start.1 = (f32[512,1024]{1,0:T(8,128)S(1)}, f32[512,1024]{1,0:T(8,128)}, u32[]{:S(2)}) copy-start(f32[512,1024]{1,0:T(8,128)} %reduce-scatter.5.cloned.1.call-done) | copy-start | bytes 6291460
Sparse Core Ops, SparseCore 0:
  119.3 10.6 reduce-scatter.2
  197.0 7.1 all-gather.7
  205.8 11.8 all-gather.5
  274.1 9.2 reduce-scatter.4
  328.9 9.1 all-gather.9
